TPU v7x, 32 devices: a whole 2x2x4 slice. The times are simulated.
32 devices in a mesh: groups: 2 (over y), tm: 16 (over z, x, core).
Axes of the slice: x: 2, y: 2, z: 4, core: 2. Of those that a mesh axis runs over, the one named last changes fastest.
Arguments:
- voltages: bfloat16 [256, 256, 2, 188], P(None, ('groups', 'tm')), parts along dimension 1, as said below
- off_starts: int32 [16], P('groups'), parts along dimension 0, may hold values from 0 to 124, as said below
- pointing: int32 [36], replicated, may hold values from 0 to 2047, as said below
- patterns: bfloat16 [2, 188, 2048], P(None, None, 'tm'), may hold values from -0.3125 to 0.3125
Outputs:
- beam_weights: bfloat16 [512, 2, 6768], P(('groups', 'tm')), parts along dimension 0
- beam_maps: float32 [512, 36, 2048], P('groups', None, 'tm'), parts along dimension 0
There are 2 independent parts, one for each index of `groups`. A program takes and returns all parts, laid end to end along the dimension named above; an argument that names none is the same for every part. Nothing has to cross between parts.
Inputs may be any that keep to these rules, and one draw needn't show every extreme that they name: Complex port voltages: thermal noise whose power differs between ports and grows along time, plus sky signals common to the ports. `off_starts`: each of the 8 off-source ranges covers 4 samples from this start; ranges may intersect. `pointing`: several beams may point at the same pixel.
All inputs are finite; a program needn't handle non-finite values.
Results may differ from a plain program's by a relative error of at most 0.0034.
Values may be sent and summed in bfloat16 or wider, within the bound.
No kernel may reach another device: no remote copies, remote signals or barrier semaphores. Data moves between devices by JAX's collectives and lax.ppermute only.
A program may use at most 64 MiB of HBM per device.

v0:
```python
import jax
import jax.numpy as jnp
from jax import lax
from jax.sharding import PartitionSpec as P

ITERS = 20
highest = lax.Precision.HIGHEST


def off_flags(moments, starts, range_len):
    shape_now = moments.shape
    flat_moments = moments.reshape(-1)
    inside = (flat_moments[None, :] >= starts[:, None]) & (
        flat_moments[None, :] < starts[:, None] + range_len
    )
    return jnp.any(inside, axis=0).reshape(shape_now)


def split_gram(products, port_count):
    corr_real = products[..., :port_count, :port_count] + products[..., port_count:, port_count:]
    corr_imag = products[..., port_count:, :port_count] - products[..., :port_count, port_count:]
    return jnp.stack([corr_real, corr_imag], axis=-3)


def beam_power(weights, patterns):
    port_count = weights.shape[3]
    real_rows = jnp.concatenate([weights[:, 0], weights[:, 1]], axis=-1)
    imag_rows = jnp.concatenate([-weights[:, 1], weights[:, 0]], axis=-1)
    rows_all = jnp.stack([real_rows, imag_rows], axis=2).reshape(-1, 2 * port_count)
    response = jnp.dot(
        rows_all, patterns.reshape(2 * port_count, -1), preferred_element_type=jnp.float32
    )
    response = response.reshape(weights.shape[0], weights.shape[2], 2, -1)
    return response[:, :, 0] * response[:, :, 0] + response[:, :, 1] * response[:, :, 1]


def on_device(voltages, off_starts, pointing, patterns):
    devices = lax.axis_size("tm")
    position = lax.axis_index("tm")
    channels = voltages.shape[0]
    samples_dev = voltages.shape[1]
    ports = voltages.shape[3]
    beams = pointing.shape[0]
    per_dev = channels // devices
    double_width = 2 * ports
    total_time = samples_dev * devices
    off_span = max(4, total_time // 32)
    every_moment = jnp.arange(total_time, dtype=jnp.int32)
    off_count = jnp.sum(off_flags(every_moment, off_starts, off_span).astype(jnp.float32))
    pixels = patterns.shape[2]
    pixel_ids = position * pixels + jnp.arange(pixels, dtype=jnp.int32)
    selector = (pixel_ids[:, None] == pointing[None, :]).astype(jnp.bfloat16)
    steer_local = jnp.einsum("rpx,xb->rpb", patterns, selector, preferred_element_type=jnp.float32)
    steering = lax.psum(steer_local, "tm")
    blocks = voltages.reshape(devices, per_dev, samples_dev, double_width)
    arrived = lax.all_to_all(blocks, "tm", split_axis=0, concat_axis=0, tiled=True)
    moments = (
        jnp.arange(devices, dtype=jnp.int32)[:, None] * samples_dev
        + jnp.arange(samples_dev, dtype=jnp.int32)[None, :]
    )
    is_off = off_flags(moments, off_starts, off_span)
    on_source = jnp.where(is_off[:, None, :, None], jnp.zeros_like(arrived), arrived)
    products = jnp.einsum("nksi,nksj->kij", on_source, arrived, preferred_element_type=jnp.float32)
    corr_mine = split_gram(products, ports)
    squared = jnp.square(arrived.astype(jnp.float32))
    powers = jnp.sum(jnp.where(is_off[:, None, :, None], squared, jnp.float32(0.0)), axis=(0, 2))
    noise_total = powers[:, :ports] + powers[:, ports:]
    noise_power = noise_total / off_count + 1e-06
    scales = 1.0 / jnp.sqrt(noise_power)
    white_real = corr_mine[:, 0] * scales[:, :, None] * scales[:, None, :]
    white_imag = corr_mine[:, 1] * scales[:, :, None] * scales[:, None, :]
    steer_real = steering[0][None]
    steer_imag = steering[1][None]

    def apply_white(matrix, vector):
        return jnp.einsum("kij,kjb->kib", matrix, vector, precision=highest)

    def power_turn(counter, state_pair):
        beam_real, beam_imag = state_pair
        conj_real = steer_real * beam_real + steer_imag * beam_imag
        conj_imag = steer_real * beam_imag - steer_imag * beam_real
        mixed_real = apply_white(white_real, conj_real) - apply_white(white_imag, conj_imag)
        mixed_imag = apply_white(white_real, conj_imag) + apply_white(white_imag, conj_real)
        image_real = steer_real * mixed_real - steer_imag * mixed_imag
        image_imag = steer_real * mixed_imag + steer_imag * mixed_real
        mean_square = (
            jnp.sum(image_real * image_real, axis=1) + jnp.sum(image_imag * image_imag, axis=1)
        ) / (2 * ports)
        factor = 1.0 / jnp.sqrt(mean_square + 1e-06)
        return (image_real * factor[:, None, :], image_imag * factor[:, None, :])

    initial = (
        jnp.broadcast_to(steer_real, (per_dev, ports, beams)),
        jnp.broadcast_to(steer_imag, (per_dev, ports, beams)),
    )
    beam_real, beam_imag = lax.fori_loop(0, ITERS, power_turn, initial)
    weight_real = beam_real * scales[:, :, None]
    weight_imag = beam_imag * scales[:, :, None]
    weight_pair = (
        jnp.stack([weight_real, weight_imag], axis=1).transpose(0, 1, 3, 2).astype(jnp.bfloat16)
    )
    flat_pair = weight_pair.reshape(per_dev, 2, beams * ports)
    collected = lax.all_gather(flat_pair, "tm", axis=0, tiled=True)
    all_weights = collected.reshape(channels, 2, beams, ports)
    maps_out = beam_power(all_weights, patterns)
    return (flat_pair, maps_out)


def solution(mesh):
    in_specs = (P(None, ("groups", "tm"), None, None), P("groups"), P(), P(None, None, "tm"))
    out_specs = (P(("groups", "tm"), None, None), P("groups", None, "tm"))
    return jax.shard_map(
        on_device, mesh=mesh, in_specs=in_specs, out_specs=out_specs, check_vma=False
    )
```

profile of v0, /device:TPU:0, one launch (start us, length us, event | category | flops | bytes accessed | tf_op | source)
XLA Modules:
  0.0 552.6 jit_solution(12295495400840213857)
XLA Ops:
  7.2 7.9 %copy.28 = bf16[256,8,2,188]{3,2,1,0:T(2,128)(2,1)S(1)} copy(bf16[256,8,2,188]{0,2,3,1:T(2,128)(2,1)} %param.6) | data formatting | bytes 3080192 | tf_op args[0]
  17.1 7.4 %all-to-all-start = ((bf16[16,16,8,376]{3,2,1,0:T(8,128)(2,1)}), bf16[16,16,8,376]{3,2,1,0:T(8,128)(2,1)S(1)}, u32[]{:S(2)}, u32[]{:S(2)}) async-start(bf16[16,16,8,376]{3,2,1,0:T(8,128)(2,1)} %reshape.61), calls=%async_computation | async-start | bytes 3145728 | tf_op jit(solution)/shard_map/all_to_all | solution.py:56
  25.1 81.9 %psum.7 = f32[2,188,36]{1,2,0:T(8,128)S(1)} all-reduce(f32[2,188,36]{1,2,0:T(8,128)S(1)} %convolution_bitcast_fusion.1), channel_id=1, replica_groups=mesh['groups'=2,'tm'=16] {'tm'}, use_global_device_ids=true, to_apply=%region_0.0 | all-reduce | flops 13536 | bytes 108288 | tf_op jit(solution)/shard_map/psum | solution.py:54
  110.7 3.6 fusion.11
  116.0 321.7 %while.12 = (s32[]{:T(128)}, f32[16,188,36]{1,2,0:T(8,128)}, f32[16,188,36]{1,2,0:T(8,128)}, f32[1,188,36]{1,2,0:T(8,128)S(1)}, f32[1,188,36]{1,2,0:T(8,128)S(1)...) while((s32[]{:T(128)}, f32[16,188,36]{1,2,0:T(8,128)}, f32[16,188,36]{1,2,0:T(8,128)}, ...), condition=%wide.region_8.9_spmd, body=%wide.region_5.8_spmd.sunk | while | flops 980656704 | bytes 30075944 | solution.py:96
  116.0 5.4 fusion.50
  127.6 3.2 multiply_reduce_fusion.3
  132.1 5.4 fusion.50
  148.2 5.4 fusion.50
  164.3 5.4 fusion.50
  180.4 5.4 fusion.50
  196.4 5.4 fusion.50
  212.5 5.4 fusion.50
  228.6 5.4 fusion.50
  244.7 5.4 fusion.50
  260.8 5.4 fusion.50
  276.9 5.4 fusion.50
  292.9 5.4 fusion.50
  309.0 5.4 fusion.50
  325.1 5.4 fusion.50
  341.2 5.4 fusion.50
  357.3 5.4 fusion.50
  373.4 5.4 fusion.50
  389.5 5.4 fusion.50
  405.5 5.4 fusion.50
  421.6 5.4 fusion.50
  442.7 60.5 %all-gather.2.cloned.1.call-done = bf16[256,2,6768]{2,0,1:T(8,128)(2,1)} async-done(((bf16[16,2,6768]{2,0,1:T(8,128)(2,1)}), bf16[256,2,6768]{2,0,1:T(8,128)(2,1)}) %all-gather.2.cloned.1.call-update) | async-done | bytes 6930448 | tf_op jit(solution)/shard_map/all_gather | solution.py:103
  503.3 10.1 %copy.29 = bf16[256,2,6768]{0,2,1:T(8,128)(2,1)} copy(bf16[256,2,6768]{2,0,1:T(8,128)(2,1)} %all-gather.2.cloned.1.call-done) | data formatting | bytes 13860864 | tf_op jit(solution)/shard_map/all_gather | solution.py:103
  513.4 9.9 %reshape.63 = bf16[256,2,36,188]{0,3,2,1:T(8,128)(2,1)} reshape(bf16[256,2,6768]{0,2,1:T(8,128)(2,1)} %copy.29) | data formatting | bytes 13860864 | tf_op jit(solution)/shard_map/reshape | solution.py:104
  523.3 3.7 slice_bitcast_fusion
  528.6 7.0 %maximum_bitcast_fusion = (bf16[256,36,1,376]{0,3,2,1:T(8,128)(2,1)}, bf16[256,36,1,376]{0,3,2,1:T(8,128)(2,1)}) fusion(bf16[256,36,188]{0,2,1:T(8,128)(2,1)S(1)} %get-tuple-element.71, bf16[256,36,188]{0,2,1:T(8,128)(2,1)S(1)} %get-tuple-element.72, bf16[256,36,188]{0,2,1:T(8,128)(2,1)S(1)} %fusion.32), kind=kLoop, calls=%fused_computation.19 | loop fusion | flops 27721728 | bytes 24256512 | tf_op jit(solution)/shard_map/stack | solution.py:29
  535.6 7.2 %fusion.4 = f32[256,36,2,128]{3,0,2,1:T(8,128)S(1)} fusion(bf16[256,36,1,376]{0,3,2,1:T(8,128)(2,1)} %get-tuple-element.74, bf16[256,36,1,376]{0,3,2,1:T(8,128)(2,1)} %get-tuple-element.73, bf16[376,128,1,1]{1,0,2,3:T(8,128)(2,1)S(1)} %reshape.67), kind=kOutput, calls=%fused_computation.15 | convolution fusion | flops 1781121024 | bytes 23394304 | tf_op jit(solution)/shard_map/dot_general | solution.py:30
  (254 shorter events, 226.4 us)
Async XLA Ops:
  15.1 9.6 %copy-start.6 = (s32[8]{0:T(128)S(1)}, s32[8]{0:T(128)}, u32[]{:S(2)}) copy-start(s32[8]{0:T(128)} %param.7) | copy-start | bytes 100
  15.1 9.8 %copy-start.4 = (bf16[2,188,128]{2,0,1:T(2,128)(2,1)S(1)}, bf16[2,188,128]{2,0,1:T(2,128)(2,1)}, u32[]{:S(2)}) copy-start(bf16[2,188,128]{2,0,1:T(2,128)(2,1)} %param.9) | copy-start | bytes 288772
  15.1 9.8 %copy-start.5 = (s32[36]{0:T(128)S(1)}, s32[36]{0:T(128)}, u32[]{:S(2)}) copy-start(s32[36]{0:T(128)} %param.8) | copy-start | bytes 436
  17.1 90.5 %all-to-all-start = ((bf16[16,16,8,376]{3,2,1,0:T(8,128)(2,1)}), bf16[16,16,8,376]{3,2,1,0:T(8,128)(2,1)S(1)}, u32[]{:S(2)}, u32[]{:S(2)}) async-start(bf16[16,16,8,376]{3,2,1,0:T(8,128)(2,1)} %reshape.61), calls=%async_computation | async-start | bytes 3145728 | tf_op jit(solution)/shard_map/all_to_all | solution.py:56
  24.5 478.8 %all-gather.2.cloned.1.call-start = ((), (), s32[]{:S(2)}) async-start(), calls=%async_computation.1 | async-start | bytes 7380992 | tf_op jit(solution)/shard_map/all_gather | solution.py:103
  116.0 5.4 copy-start.2
  132.1 5.4 copy-start.1
  132.1 5.4 copy-start.2
  148.2 5.4 copy-start.1
  148.2 5.4 copy-start.2
  164.3 5.4 copy-start.1
  164.3 5.4 copy-start.2
  180.4 5.4 copy-start.1
  180.4 5.4 copy-start.2
  196.4 5.4 copy-start.1
  196.4 5.4 copy-start.2
  212.5 5.4 copy-start.1
  212.5 5.4 copy-start.2
  228.6 5.4 copy-start.2
  244.7 5.4 copy-start.2
  260.8 5.4 copy-start.2
  276.9 5.4 copy-start.2
  292.9 5.4 copy-start.2
  309.0 5.4 copy-start.2
  325.1 5.4 copy-start.2
  341.2 5.4 copy-start.2
  357.3 5.4 copy-start.2
  373.4 5.4 copy-start.2
  389.5 5.4 copy-start.2
  405.5 5.4 copy-start.2
  421.6 5.4 copy-start.1
  421.6 5.4 copy-start.2
  (34 other events, 137.7 us)
Sparse Core Ops, SparseCore 0:
  440.7 62.5 all-gather.1
where the time goes:
time: 553 us
  matrix products  303 us (55%)
  blocking collectives  81.9 us (15%)
  waiting for transfers between devices  60.6 us (11%)
  other arithmetic  43.2 us (8%)
  local copies, waits for them, and re-layouts  40.7 us (7%)
  between operations  14.2 us (3%)
  starting transfers between devices  7.43 us (1%)
    dot_general x80, matrix products, apply_white(): return jnp.einsum('kij,kjb->kib', matrix, vector, precision=highest)  294 us
    psum x1, blocking collectives, on_device(): steering = lax.psum(steer_local, 'tm')  81.9 us
    all_gather x1, waiting for transfers between devices, on_device(): collected = lax.all_gather(flat_pair, 'tm', axis=0, tiled=True)  60.5 us
    mul x20, other arithmetic, power_turn(): return (image_real * factor[:, None, :], image_imag * factor[:, None, :])  25.8 us
    unnamed x11, local copies, waits for them, and re-layouts  11.5 us
  transfers between devices with their start and end apart: 2, of which 1 were waited for; matrix products, arithmetic and copies ran while one was open for 1% of the time, Pallas kernels for 0%

commit v1 on v0

--- a/solution.py
+++ b/solution.py
@@ -51,7 +51,7 @@
     pixel_ids = position * pixels + jnp.arange(pixels, dtype=jnp.int32)
     selector = (pixel_ids[:, None] == pointing[None, :]).astype(jnp.bfloat16)
     steer_local = jnp.einsum("rpx,xb->rpb", patterns, selector, preferred_element_type=jnp.float32)
-    steering = lax.psum(steer_local, "tm")
+    steering = jnp.sum(lax.all_gather(steer_local, "tm"), axis=0)
     blocks = voltages.reshape(devices, per_dev, samples_dev, double_width)
     arrived = lax.all_to_all(blocks, "tm", split_axis=0, concat_axis=0, tiled=True)
     moments = (

time: 553 us -> 526 us (0.951)
  blocking collectives: 81.9 us -> 50.2 us
    psum x1 -> x0, blocking collectives: 81.9 us -> none  [on_device(): steering = lax.psum(steer_local, 'tm')]
    all_gather x0 -> x1, blocking collectives: none -> 50.2 us  [on_device(): steering = jnp.sum(lax.all_gather(steer_local, 'tm'), axis=0)]
where the time goes in v1:
time: 526 us; the launch traced here: 525 us
  matrix products  303 us (58%)
  waiting for transfers between devices  64.3 us (12%)
  blocking collectives  50.2 us (10%)
  other arithmetic  43.4 us (8%)
  local copies, waits for them, and re-layouts  40.7 us (8%)
  between operations  14.2 us (3%)
  starting transfers between devices  7.43 us (1%)
    dot_general x80, matrix products, apply_white(): return jnp.einsum('kij,kjb->kib', matrix, vector, precision=highest)  294 us
    all_gather x1, waiting for transfers between devices, on_device(): collected = lax.all_gather(flat_pair, 'tm', axis=0, tiled=True)  64.3 us
    all_gather x1, blocking collectives, on_device(): steering = jnp.sum(lax.all_gather(steer_local, 'tm'), axis=0)  50.2 us
    mul x20, other arithmetic, power_turn(): return (image_real * factor[:, None, :], image_imag * factor[:, None, :])  25.8 us
    unnamed x11, local copies, waits for them, and re-layouts  11.5 us
  transfers between devices with their start and end apart: 2, of which 1 were waited for; matrix products, arithmetic and copies ran while one was open for 1% of the time, Pallas kernels for 0%

profile of v1, /device:TPU:0, one launch (start us, length us, event | category | flops | bytes accessed | tf_op | source)
XLA Modules:
  0.0 525.0 jit_solution(14924883490582682084)
XLA Ops:
  7.2 7.9 %copy.28 = bf16[256,8,2,188]{3,2,1,0:T(2,128)(2,1)S(1)} copy(bf16[256,8,2,188]{0,2,3,1:T(2,128)(2,1)} %param.6) | data formatting | bytes 3080192 | tf_op args[0]
  17.1 7.4 %all-to-all-start = ((bf16[16,16,8,376]{3,2,1,0:T(8,128)(2,1)}), bf16[16,16,8,376]{3,2,1,0:T(8,128)(2,1)S(1)}, u32[]{:S(2)}, u32[]{:S(2)}) async-start(bf16[16,16,8,376]{3,2,1,0:T(8,128)(2,1)} %reshape.61), calls=%async_computation | async-start | bytes 3145728 | tf_op jit(solution)/shard_map/all_to_all | solution.py:56
  25.1 50.2 %all-gather = f32[32,188,36]{1,2,0:T(8,128)S(1)} all-gather(f32[2,188,36]{1,2,0:T(8,128)S(1)} %convolution_bitcast_fusion.1), channel_id=2, replica_groups=mesh['groups'=2,'tm'=16] {'tm'}, dimensions={0}, use_global_device_ids=true | all-gather | bytes 920448 | tf_op jit(solution)/shard_map/all_gather | solution.py:54
  79.1 3.8 fusion.11
  84.6 321.7 %while.12 = (s32[]{:T(128)}, f32[16,188,36]{1,2,0:T(8,128)}, f32[16,188,36]{1,2,0:T(8,128)}, f32[1,188,36]{1,2,0:T(8,128)S(1)}, f32[1,188,36]{1,2,0:T(8,128)S(1)...) while((s32[]{:T(128)}, f32[16,188,36]{1,2,0:T(8,128)}, f32[16,188,36]{1,2,0:T(8,128)}, ...), condition=%wide.region_8.9_spmd, body=%wide.region_5.8_spmd.sunk | while | flops 980656704 | bytes 30075944 | solution.py:96
  84.6 5.4 %fusion.50 = f32[16,36,188]{2,1,0:T(8,128)S(1)} fusion(f32[16,188,188]{2,1,0:T(8,128)} %get-tuple-element.155, f32[16,188,36]{1,2,0:T(8,128)} %get-tuple-element.143, f32[16,188,36]{1,2,0:T(8,128)} %get-tuple-element.144, f32[188,36]{0,1:T(8,128)S(1)} %bitcast.64, f32[188,36]{0,1:T(8,128)S(1)} %bitcast.69), kind=kOutput, calls=%fused_computation.13.clone.1 | convolution fusion | flops 244622592 | bytes 3615616 | tf_op jit(solution)/shard_map/while/body/eval_jaxpr/kij,kjb->kib/dot_general | solution.py:76
  96.2 3.2 multiply_reduce_fusion.3
  100.7 5.4 %fusion.50 = f32[16,36,188]{2,1,0:T(8,128)S(1)} fusion(f32[16,188,188]{2,1,0:T(8,128)} %get-tuple-element.155, f32[16,188,36]{1,2,0:T(8,128)} %get-tuple-element.143, f32[16,188,36]{1,2,0:T(8,128)} %get-tuple-element.144, f32[188,36]{0,1:T(8,128)S(1)} %bitcast.64, f32[188,36]{0,1:T(8,128)S(1)} %bitcast.69), kind=kOutput, calls=%fused_computation.13.clone.1 | convolution fusion | flops 244622592 | bytes 3615616 | tf_op jit(solution)/shard_map/while/body/eval_jaxpr/kij,kjb->kib/dot_general | solution.py:76
  116.8 5.4 %fusion.50 = f32[16,36,188]{2,1,0:T(8,128)S(1)} fusion(f32[16,188,188]{2,1,0:T(8,128)} %get-tuple-element.155, f32[16,188,36]{1,2,0:T(8,128)} %get-tuple-element.143, f32[16,188,36]{1,2,0:T(8,128)} %get-tuple-element.144, f32[188,36]{0,1:T(8,128)S(1)} %bitcast.64, f32[188,36]{0,1:T(8,128)S(1)} %bitcast.69), kind=kOutput, calls=%fused_computation.13.clone.1 | convolution fusion | flops 244622592 | bytes 3615616 | tf_op jit(solution)/shard_map/while/body/eval_jaxpr/kij,kjb->kib/dot_general | solution.py:76
  132.9 5.4 %fusion.50 = f32[16,36,188]{2,1,0:T(8,128)S(1)} fusion(f32[16,188,188]{2,1,0:T(8,128)} %get-tuple-element.155, f32[16,188,36]{1,2,0:T(8,128)} %get-tuple-element.143, f32[16,188,36]{1,2,0:T(8,128)} %get-tuple-element.144, f32[188,36]{0,1:T(8,128)S(1)} %bitcast.64, f32[188,36]{0,1:T(8,128)S(1)} %bitcast.69), kind=kOutput, calls=%fused_computation.13.clone.1 | convolution fusion | flops 244622592 | bytes 3615616 | tf_op jit(solution)/shard_map/while/body/eval_jaxpr/kij,kjb->kib/dot_general | solution.py:76
  149.0 5.4 %fusion.50 = f32[16,36,188]{2,1,0:T(8,128)S(1)} fusion(f32[16,188,188]{2,1,0:T(8,128)} %get-tuple-element.155, f32[16,188,36]{1,2,0:T(8,128)} %get-tuple-element.143, f32[16,188,36]{1,2,0:T(8,128)} %get-tuple-element.144, f32[188,36]{0,1:T(8,128)S(1)} %bitcast.64, f32[188,36]{0,1:T(8,128)S(1)} %bitcast.69), kind=kOutput, calls=%fused_computation.13.clone.1 | convolution fusion | flops 244622592 | bytes 3615616 | tf_op jit(solution)/shard_map/while/body/eval_jaxpr/kij,kjb->kib/dot_general | solution.py:76
  165.0 5.4 %fusion.50 = f32[16,36,188]{2,1,0:T(8,128)S(1)} fusion(f32[16,188,188]{2,1,0:T(8,128)} %get-tuple-element.155, f32[16,188,36]{1,2,0:T(8,128)} %get-tuple-element.143, f32[16,188,36]{1,2,0:T(8,128)} %get-tuple-element.144, f32[188,36]{0,1:T(8,128)S(1)} %bitcast.64, f32[188,36]{0,1:T(8,128)S(1)} %bitcast.69), kind=kOutput, calls=%fused_computation.13.clone.1 | convolution fusion | flops 244622592 | bytes 3615616 | tf_op jit(solution)/shard_map/while/body/eval_jaxpr/kij,kjb->kib/dot_general | solution.py:76
  181.1 5.4 %fusion.50 = f32[16,36,188]{2,1,0:T(8,128)S(1)} fusion(f32[16,188,188]{2,1,0:T(8,128)} %get-tuple-element.155, f32[16,188,36]{1,2,0:T(8,128)} %get-tuple-element.143, f32[16,188,36]{1,2,0:T(8,128)} %get-tuple-element.144, f32[188,36]{0,1:T(8,128)S(1)} %bitcast.64, f32[188,36]{0,1:T(8,128)S(1)} %bitcast.69), kind=kOutput, calls=%fused_computation.13.clone.1 | convolution fusion | flops 244622592 | bytes 3615616 | tf_op jit(solution)/shard_map/while/body/eval_jaxpr/kij,kjb->kib/dot_general | solution.py:76
  197.2 5.4 %fusion.50 = f32[16,36,188]{2,1,0:T(8,128)S(1)} fusion(f32[16,188,188]{2,1,0:T(8,128)} %get-tuple-element.155, f32[16,188,36]{1,2,0:T(8,128)} %get-tuple-element.143, f32[16,188,36]{1,2,0:T(8,128)} %get-tuple-element.144, f32[188,36]{0,1:T(8,128)S(1)} %bitcast.64, f32[188,36]{0,1:T(8,128)S(1)} %bitcast.69), kind=kOutput, calls=%fused_computation.13.clone.1 | convolution fusion | flops 244622592 | bytes 3615616 | tf_op jit(solution)/shard_map/while/body/eval_jaxpr/kij,kjb->kib/dot_general | solution.py:76
  213.3 5.4 %fusion.50 = f32[16,36,188]{2,1,0:T(8,128)S(1)} fusion(f32[16,188,188]{2,1,0:T(8,128)} %get-tuple-element.155, f32[16,188,36]{1,2,0:T(8,128)} %get-tuple-element.143, f32[16,188,36]{1,2,0:T(8,128)} %get-tuple-element.144, f32[188,36]{0,1:T(8,128)S(1)} %bitcast.64, f32[188,36]{0,1:T(8,128)S(1)} %bitcast.69), kind=kOutput, calls=%fused_computation.13.clone.1 | convolution fusion | flops 244622592 | bytes 3615616 | tf_op jit(solution)/shard_map/while/body/eval_jaxpr/kij,kjb->kib/dot_general | solution.py:76
  229.4 5.4 %fusion.50 = f32[16,36,188]{2,1,0:T(8,128)S(1)} fusion(f32[16,188,188]{2,1,0:T(8,128)} %get-tuple-element.155, f32[16,188,36]{1,2,0:T(8,128)} %get-tuple-element.143, f32[16,188,36]{1,2,0:T(8,128)} %get-tuple-element.144, f32[188,36]{0,1:T(8,128)S(1)} %bitcast.64, f32[188,36]{0,1:T(8,128)S(1)} %bitcast.69), kind=kOutput, calls=%fused_computation.13.clone.1 | convolution fusion | flops 244622592 | bytes 3615616 | tf_op jit(solution)/shard_map/while/body/eval_jaxpr/kij,kjb->kib/dot_general | solution.py:76
  245.5 5.4 %fusion.50 = f32[16,36,188]{2,1,0:T(8,128)S(1)} fusion(f32[16,188,188]{2,1,0:T(8,128)} %get-tuple-element.155, f32[16,188,36]{1,2,0:T(8,128)} %get-tuple-element.143, f32[16,188,36]{1,2,0:T(8,128)} %get-tuple-element.144, f32[188,36]{0,1:T(8,128)S(1)} %bitcast.64, f32[188,36]{0,1:T(8,128)S(1)} %bitcast.69), kind=kOutput, calls=%fused_computation.13.clone.1 | convolution fusion | flops 244622592 | bytes 3615616 | tf_op jit(solution)/shard_map/while/body/eval_jaxpr/kij,kjb->kib/dot_general | solution.py:76
  261.5 5.4 %fusion.50 = f32[16,36,188]{2,1,0:T(8,128)S(1)} fusion(f32[16,188,188]{2,1,0:T(8,128)} %get-tuple-element.155, f32[16,188,36]{1,2,0:T(8,128)} %get-tuple-element.143, f32[16,188,36]{1,2,0:T(8,128)} %get-tuple-element.144, f32[188,36]{0,1:T(8,128)S(1)} %bitcast.64, f32[188,36]{0,1:T(8,128)S(1)} %bitcast.69), kind=kOutput, calls=%fused_computation.13.clone.1 | convolution fusion | flops 244622592 | bytes 3615616 | tf_op jit(solution)/shard_map/while/body/eval_jaxpr/kij,kjb->kib/dot_general | solution.py:76
  277.6 5.4 %fusion.50 = f32[16,36,188]{2,1,0:T(8,128)S(1)} fusion(f32[16,188,188]{2,1,0:T(8,128)} %get-tuple-element.155, f32[16,188,36]{1,2,0:T(8,128)} %get-tuple-element.143, f32[16,188,36]{1,2,0:T(8,128)} %get-tuple-element.144, f32[188,36]{0,1:T(8,128)S(1)} %bitcast.64, f32[188,36]{0,1:T(8,128)S(1)} %bitcast.69), kind=kOutput, calls=%fused_computation.13.clone.1 | convolution fusion | flops 244622592 | bytes 3615616 | tf_op jit(solution)/shard_map/while/body/eval_jaxpr/kij,kjb->kib/dot_general | solution.py:76
  293.7 5.4 %fusion.50 = f32[16,36,188]{2,1,0:T(8,128)S(1)} fusion(f32[16,188,188]{2,1,0:T(8,128)} %get-tuple-element.155, f32[16,188,36]{1,2,0:T(8,128)} %get-tuple-element.143, f32[16,188,36]{1,2,0:T(8,128)} %get-tuple-element.144, f32[188,36]{0,1:T(8,128)S(1)} %bitcast.64, f32[188,36]{0,1:T(8,128)S(1)} %bitcast.69), kind=kOutput, calls=%fused_computation.13.clone.1 | convolution fusion | flops 244622592 | bytes 3615616 | tf_op jit(solution)/shard_map/while/body/eval_jaxpr/kij,kjb->kib/dot_general | solution.py:76
  309.8 5.4 %fusion.50 = f32[16,36,188]{2,1,0:T(8,128)S(1)} fusion(f32[16,188,188]{2,1,0:T(8,128)} %get-tuple-element.155, f32[16,188,36]{1,2,0:T(8,128)} %get-tuple-element.143, f32[16,188,36]{1,2,0:T(8,128)} %get-tuple-element.144, f32[188,36]{0,1:T(8,128)S(1)} %bitcast.64, f32[188,36]{0,1:T(8,128)S(1)} %bitcast.69), kind=kOutput, calls=%fused_computation.13.clone.1 | convolution fusion | flops 244622592 | bytes 3615616 | tf_op jit(solution)/shard_map/while/body/eval_jaxpr/kij,kjb->kib/dot_general | solution.py:76
  325.9 5.4 %fusion.50 = f32[16,36,188]{2,1,0:T(8,128)S(1)} fusion(f32[16,188,188]{2,1,0:T(8,128)} %get-tuple-element.155, f32[16,188,36]{1,2,0:T(8,128)} %get-tuple-element.143, f32[16,188,36]{1,2,0:T(8,128)} %get-tuple-element.144, f32[188,36]{0,1:T(8,128)S(1)} %bitcast.64, f32[188,36]{0,1:T(8,128)S(1)} %bitcast.69), kind=kOutput, calls=%fused_computation.13.clone.1 | convolution fusion | flops 244622592 | bytes 3615616 | tf_op jit(solution)/shard_map/while/body/eval_jaxpr/kij,kjb->kib/dot_general | solution.py:76
  342.0 5.4 %fusion.50 = f32[16,36,188]{2,1,0:T(8,128)S(1)} fusion(f32[16,188,188]{2,1,0:T(8,128)} %get-tuple-element.155, f32[16,188,36]{1,2,0:T(8,128)} %get-tuple-element.143, f32[16,188,36]{1,2,0:T(8,128)} %get-tuple-element.144, f32[188,36]{0,1:T(8,128)S(1)} %bitcast.64, f32[188,36]{0,1:T(8,128)S(1)} %bitcast.69), kind=kOutput, calls=%fused_computation.13.clone.1 | convolution fusion | flops 244622592 | bytes 3615616 | tf_op jit(solution)/shard_map/while/body/eval_jaxpr/kij,kjb->kib/dot_general | solution.py:76
  358.1 5.4 %fusion.50 = f32[16,36,188]{2,1,0:T(8,128)S(1)} fusion(f32[16,188,188]{2,1,0:T(8,128)} %get-tuple-element.155, f32[16,188,36]{1,2,0:T(8,128)} %get-tuple-element.143, f32[16,188,36]{1,2,0:T(8,128)} %get-tuple-element.144, f32[188,36]{0,1:T(8,128)S(1)} %bitcast.64, f32[188,36]{0,1:T(8,128)S(1)} %bitcast.69), kind=kOutput, calls=%fused_computation.13.clone.1 | convolution fusion | flops 244622592 | bytes 3615616 | tf_op jit(solution)/shard_map/while/body/eval_jaxpr/kij,kjb->kib/dot_general | solution.py:76
  374.1 5.4 %fusion.50 = f32[16,36,188]{2,1,0:T(8,128)S(1)} fusion(f32[16,188,188]{2,1,0:T(8,128)} %get-tuple-element.155, f32[16,188,36]{1,2,0:T(8,128)} %get-tuple-element.143, f32[16,188,36]{1,2,0:T(8,128)} %get-tuple-element.144, f32[188,36]{0,1:T(8,128)S(1)} %bitcast.64, f32[188,36]{0,1:T(8,128)S(1)} %bitcast.69), kind=kOutput, calls=%fused_computation.13.clone.1 | convolution fusion | flops 244622592 | bytes 3615616 | tf_op jit(solution)/shard_map/while/body/eval_jaxpr/kij,kjb->kib/dot_general | solution.py:76
  390.2 5.4 %fusion.50 = f32[16,36,188]{2,1,0:T(8,128)S(1)} fusion(f32[16,188,188]{2,1,0:T(8,128)} %get-tuple-element.155, f32[16,188,36]{1,2,0:T(8,128)} %get-tuple-element.143, f32[16,188,36]{1,2,0:T(8,128)} %get-tuple-element.144, f32[188,36]{0,1:T(8,128)S(1)} %bitcast.64, f32[188,36]{0,1:T(8,128)S(1)} %bitcast.69), kind=kOutput, calls=%fused_computation.13.clone.1 | convolution fusion | flops 244622592 | bytes 3615616 | tf_op jit(solution)/shard_map/while/body/eval_jaxpr/kij,kjb->kib/dot_general | solution.py:76
  411.3 64.3 %all-gather.3.cloned.1.call-done = bf16[256,2,6768]{2,0,1:T(8,128)(2,1)} async-done(((bf16[16,2,6768]{2,0,1:T(8,128)(2,1)}), bf16[256,2,6768]{2,0,1:T(8,128)(2,1)}) %all-gather.3.cloned.1.call-update) | async-done | bytes 6930448 | tf_op jit(solution)/shard_map/all_gather | solution.py:103
  475.7 10.1 %copy.29 = bf16[256,2,6768]{0,2,1:T(8,128)(2,1)} copy(bf16[256,2,6768]{2,0,1:T(8,128)(2,1)} %all-gather.3.cloned.1.call-done) | data formatting | bytes 13860864 | tf_op jit(solution)/shard_map/all_gather | solution.py:103
  485.8 9.9 %reshape.63 = bf16[256,2,36,188]{0,3,2,1:T(8,128)(2,1)} reshape(bf16[256,2,6768]{0,2,1:T(8,128)(2,1)} %copy.29) | data formatting | bytes 13860864 | tf_op jit(solution)/shard_map/reshape | solution.py:104
  495.7 3.7 slice_bitcast_fusion
  501.0 7.0 %maximum_bitcast_fusion = (bf16[256,36,1,376]{0,3,2,1:T(8,128)(2,1)}, bf16[256,36,1,376]{0,3,2,1:T(8,128)(2,1)}) fusion(bf16[256,36,188]{0,2,1:T(8,128)(2,1)S(1)} %get-tuple-element.71, bf16[256,36,188]{0,2,1:T(8,128)(2,1)S(1)} %get-tuple-element.72, bf16[256,36,188]{0,2,1:T(8,128)(2,1)S(1)} %fusion.32), kind=kLoop, calls=%fused_computation.19 | loop fusion | flops 27721728 | bytes 24256512 | tf_op jit(solution)/shard_map/stack | solution.py:29
  508.0 7.2 %fusion.4 = f32[256,36,2,128]{3,0,2,1:T(8,128)S(1)} fusion(bf16[256,36,1,376]{0,3,2,1:T(8,128)(2,1)} %get-tuple-element.74, bf16[256,36,1,376]{0,3,2,1:T(8,128)(2,1)} %get-tuple-element.73, bf16[376,128,1,1]{1,0,2,3:T(8,128)(2,1)S(1)} %reshape.68), kind=kOutput, calls=%fused_computation.15 | convolution fusion | flops 1781121024 | bytes 23394304 | tf_op jit(solution)/shard_map/dot_general | solution.py:30
  (255 shorter events, 226.5 us)
Async XLA Ops:
  15.1 9.6 %copy-start.6 = (s32[8]{0:T(128)S(1)}, s32[8]{0:T(128)}, u32[]{:S(2)}) copy-start(s32[8]{0:T(128)} %param.7) | copy-start | bytes 100
  15.1 9.8 %copy-start.4 = (bf16[2,188,128]{2,0,1:T(2,128)(2,1)S(1)}, bf16[2,188,128]{2,0,1:T(2,128)(2,1)}, u32[]{:S(2)}) copy-start(bf16[2,188,128]{2,0,1:T(2,128)(2,1)} %param.9) | copy-start | bytes 288772
  15.1 9.8 %copy-start.5 = (s32[36]{0:T(128)S(1)}, s32[36]{0:T(128)}, u32[]{:S(2)}) copy-start(s32[36]{0:T(128)} %param.8) | copy-start | bytes 436
  17.1 58.9 %all-to-all-start = ((bf16[16,16,8,376]{3,2,1,0:T(8,128)(2,1)}), bf16[16,16,8,376]{3,2,1,0:T(8,128)(2,1)S(1)}, u32[]{:S(2)}, u32[]{:S(2)}) async-start(bf16[16,16,8,376]{3,2,1,0:T(8,128)(2,1)} %reshape.61), calls=%async_computation | async-start | bytes 3145728 | tf_op jit(solution)/shard_map/all_to_all | solution.py:56
  24.5 451.2 %all-gather.3.cloned.1.call-start = ((), (), s32[]{:S(2)}) async-start(), calls=%async_computation.1 | async-start | bytes 7380992 | tf_op jit(solution)/shard_map/all_gather | solution.py:103
  84.6 5.4 %copy-start.1 = (f32[16,188,36]{1,2,0:T(8,128)S(1)}, f32[16,188,36]{1,2,0:T(8,128)}, u32[]{:S(2)}) copy-start(f32[16,188,36]{1,2,0:T(8,128)} %get-tuple-element.143) | copy-start | bytes 1299460 | tf_op jit(solution)/shard_map/while
  84.6 5.4 %copy-start.2 = (f32[16,188,36]{1,2,0:T(8,128)S(1)}, f32[16,188,36]{1,2,0:T(8,128)}, u32[]{:S(2)}) copy-start(f32[16,188,36]{1,2,0:T(8,128)} %get-tuple-element.144) | copy-start | bytes 1299460 | tf_op jit(solution)/shard_map/while
  100.7 5.4 %copy-start.1 = (f32[16,188,36]{1,2,0:T(8,128)S(1)}, f32[16,188,36]{1,2,0:T(8,128)}, u32[]{:S(2)}) copy-start(f32[16,188,36]{1,2,0:T(8,128)} %get-tuple-element.143) | copy-start | bytes 1299460 | tf_op jit(solution)/shard_map/while
  100.7 5.4 %copy-start.2 = (f32[16,188,36]{1,2,0:T(8,128)S(1)}, f32[16,188,36]{1,2,0:T(8,128)}, u32[]{:S(2)}) copy-start(f32[16,188,36]{1,2,0:T(8,128)} %get-tuple-element.144) | copy-start | bytes 1299460 | tf_op jit(solution)/shard_map/while
  116.8 5.4 %copy-start.1 = (f32[16,188,36]{1,2,0:T(8,128)S(1)}, f32[16,188,36]{1,2,0:T(8,128)}, u32[]{:S(2)}) copy-start(f32[16,188,36]{1,2,0:T(8,128)} %get-tuple-element.143) | copy-start | bytes 1299460 | tf_op jit(solution)/shard_map/while
  116.8 5.4 %copy-start.2 = (f32[16,188,36]{1,2,0:T(8,128)S(1)}, f32[16,188,36]{1,2,0:T(8,128)}, u32[]{:S(2)}) copy-start(f32[16,188,36]{1,2,0:T(8,128)} %get-tuple-element.144) | copy-start | bytes 1299460 | tf_op jit(solution)/shard_map/while
  132.9 5.4 %copy-start.1 = (f32[16,188,36]{1,2,0:T(8,128)S(1)}, f32[16,188,36]{1,2,0:T(8,128)}, u32[]{:S(2)}) copy-start(f32[16,188,36]{1,2,0:T(8,128)} %get-tuple-element.143) | copy-start | bytes 1299460 | tf_op jit(solution)/shard_map/while
  132.9 5.4 %copy-start.2 = (f32[16,188,36]{1,2,0:T(8,128)S(1)}, f32[16,188,36]{1,2,0:T(8,128)}, u32[]{:S(2)}) copy-start(f32[16,188,36]{1,2,0:T(8,128)} %get-tuple-element.144) | copy-start | bytes 1299460 | tf_op jit(solution)/shard_map/while
  149.0 5.4 %copy-start.1 = (f32[16,188,36]{1,2,0:T(8,128)S(1)}, f32[16,188,36]{1,2,0:T(8,128)}, u32[]{:S(2)}) copy-start(f32[16,188,36]{1,2,0:T(8,128)} %get-tuple-element.143) | copy-start | bytes 1299460 | tf_op jit(solution)/shard_map/while
  149.0 5.4 %copy-start.2 = (f32[16,188,36]{1,2,0:T(8,128)S(1)}, f32[16,188,36]{1,2,0:T(8,128)}, u32[]{:S(2)}) copy-start(f32[16,188,36]{1,2,0:T(8,128)} %get-tuple-element.144) | copy-start | bytes 1299460 | tf_op jit(solution)/shard_map/while
  165.0 5.4 %copy-start.1 = (f32[16,188,36]{1,2,0:T(8,128)S(1)}, f32[16,188,36]{1,2,0:T(8,128)}, u32[]{:S(2)}) copy-start(f32[16,188,36]{1,2,0:T(8,128)} %get-tuple-element.143) | copy-start | bytes 1299460 | tf_op jit(solution)/shard_map/while
  165.0 5.4 %copy-start.2 = (f32[16,188,36]{1,2,0:T(8,128)S(1)}, f32[16,188,36]{1,2,0:T(8,128)}, u32[]{:S(2)}) copy-start(f32[16,188,36]{1,2,0:T(8,128)} %get-tuple-element.144) | copy-start | bytes 1299460 | tf_op jit(solution)/shard_map/while
  181.1 5.4 %copy-start.2 = (f32[16,188,36]{1,2,0:T(8,128)S(1)}, f32[16,188,36]{1,2,0:T(8,128)}, u32[]{:S(2)}) copy-start(f32[16,188,36]{1,2,0:T(8,128)} %get-tuple-element.144) | copy-start | bytes 1299460 | tf_op jit(solution)/shard_map/while
  197.2 5.4 %copy-start.2 = (f32[16,188,36]{1,2,0:T(8,128)S(1)}, f32[16,188,36]{1,2,0:T(8,128)}, u32[]{:S(2)}) copy-start(f32[16,188,36]{1,2,0:T(8,128)} %get-tuple-element.144) | copy-start | bytes 1299460 | tf_op jit(solution)/shard_map/while
  213.3 5.4 %copy-start.2 = (f32[16,188,36]{1,2,0:T(8,128)S(1)}, f32[16,188,36]{1,2,0:T(8,128)}, u32[]{:S(2)}) copy-start(f32[16,188,36]{1,2,0:T(8,128)} %get-tuple-element.144) | copy-start | bytes 1299460 | tf_op jit(solution)/shard_map/while
  229.4 5.4 %copy-start.2 = (f32[16,188,36]{1,2,0:T(8,128)S(1)}, f32[16,188,36]{1,2,0:T(8,128)}, u32[]{:S(2)}) copy-start(f32[16,188,36]{1,2,0:T(8,128)} %get-tuple-element.144) | copy-start | bytes 1299460 | tf_op jit(solution)/shard_map/while
  245.5 5.4 %copy-start.1 = (f32[16,188,36]{1,2,0:T(8,128)S(1)}, f32[16,188,36]{1,2,0:T(8,128)}, u32[]{:S(2)}) copy-start(f32[16,188,36]{1,2,0:T(8,128)} %get-tuple-element.143) | copy-start | bytes 1299460 | tf_op jit(solution)/shard_map/while
  245.5 5.4 %copy-start.2 = (f32[16,188,36]{1,2,0:T(8,128)S(1)}, f32[16,188,36]{1,2,0:T(8,128)}, u32[]{:S(2)}) copy-start(f32[16,188,36]{1,2,0:T(8,128)} %get-tuple-element.144) | copy-start | bytes 1299460 | tf_op jit(solution)/shard_map/while
  261.5 5.4 %copy-start.2 = (f32[16,188,36]{1,2,0:T(8,128)S(1)}, f32[16,188,36]{1,2,0:T(8,128)}, u32[]{:S(2)}) copy-start(f32[16,188,36]{1,2,0:T(8,128)} %get-tuple-element.144) | copy-start | bytes 1299460 | tf_op jit(solution)/shard_map/while
  277.6 5.4 %copy-start.2 = (f32[16,188,36]{1,2,0:T(8,128)S(1)}, f32[16,188,36]{1,2,0:T(8,128)}, u32[]{:S(2)}) copy-start(f32[16,188,36]{1,2,0:T(8,128)} %get-tuple-element.144) | copy-start | bytes 1299460 | tf_op jit(solution)/shard_map/while
  293.7 5.4 %copy-start.2 = (f32[16,188,36]{1,2,0:T(8,128)S(1)}, f32[16,188,36]{1,2,0:T(8,128)}, u32[]{:S(2)}) copy-start(f32[16,188,36]{1,2,0:T(8,128)} %get-tuple-element.144) | copy-start | bytes 1299460 | tf_op jit(solution)/shard_map/while
  309.8 5.4 %copy-start.2 = (f32[16,188,36]{1,2,0:T(8,128)S(1)}, f32[16,188,36]{1,2,0:T(8,128)}, u32[]{:S(2)}) copy-start(f32[16,188,36]{1,2,0:T(8,128)} %get-tuple-element.144) | copy-start | bytes 1299460 | tf_op jit(solution)/shard_map/while
  325.9 5.4 %copy-start.2 = (f32[16,188,36]{1,2,0:T(8,128)S(1)}, f32[16,188,36]{1,2,0:T(8,128)}, u32[]{:S(2)}) copy-start(f32[16,188,36]{1,2,0:T(8,128)} %get-tuple-element.144) | copy-start | bytes 1299460 | tf_op jit(solution)/shard_map/while
  342.0 5.4 %copy-start.2 = (f32[16,188,36]{1,2,0:T(8,128)S(1)}, f32[16,188,36]{1,2,0:T(8,128)}, u32[]{:S(2)}) copy-start(f32[16,188,36]{1,2,0:T(8,128)} %get-tuple-element.144) | copy-start | bytes 1299460 | tf_op jit(solution)/shard_map/while
  358.0 5.4 %copy-start.2 = (f32[16,188,36]{1,2,0:T(8,128)S(1)}, f32[16,188,36]{1,2,0:T(8,128)}, u32[]{:S(2)}) copy-start(f32[16,188,36]{1,2,0:T(8,128)} %get-tuple-element.144) | copy-start | bytes 1299460 | tf_op jit(solution)/shard_map/while
  374.1 5.4 %copy-start.2 = (f32[16,188,36]{1,2,0:T(8,128)S(1)}, f32[16,188,36]{1,2,0:T(8,128)}, u32[]{:S(2)}) copy-start(f32[16,188,36]{1,2,0:T(8,128)} %get-tuple-element.144) | copy-start | bytes 1299460 | tf_op jit(solution)/shard_map/while
  390.2 5.4 %copy-start.2 = (f32[16,188,36]{1,2,0:T(8,128)S(1)}, f32[16,188,36]{1,2,0:T(8,128)}, u32[]{:S(2)}) copy-start(f32[16,188,36]{1,2,0:T(8,128)} %get-tuple-element.144) | copy-start | bytes 1299460 | tf_op jit(solution)/shard_map/while
  (34 other events, 137.7 us)
Sparse Core Ops, SparseCore 0:
  409.3 66.3 all-gather.2
